TPU v7x, 32 devices: a whole 2x2x4 slice. The times are simulated.
32 devices in a mesh: req: 8 (over z, x), mlp: 4 (over y, core).
Axes of the slice: x: 2, y: 2, z: 4, core: 2. Of those that a mesh axis runs over, the one named last changes fastest.
Arguments:
- tokens: bfloat16 [8192, 2048], P('req'), may hold values from -6 to 6
- first_gain: float32 [2048], replicated, may hold values from 0.5 to 1.5
- joined_weight: bfloat16 [2048, 6144], P(None, 'mlp'), may hold values from -0.125 to 0.125
- dense_weight: bfloat16 [2048, 2048], P('mlp'), may hold values from -0.125 to 0.125
- adapter_down: bfloat16 [64, 16, 2048], P('req', None, 'mlp'), may hold values from -0.125 to 0.125
- adapter_up: bfloat16 [64, 16, 2048], P('req'), may hold values from -1.5 to 1.5
- adapter_ids: int32 [64], replicated, may hold values from 0 to 63, as said below
- adapter_rows: int32 [64], replicated, may hold values from 0 to 63, each once
- second_gain: float32 [2048], replicated, may hold values from 0.5 to 1.5
- up_weight: bfloat16 [2048, 8192], P(None, 'mlp'), may hold values from -0.125 to 0.125
- down_weight: bfloat16 [8192, 2048], P('mlp'), may hold values from -0.0625 to 0.0625
- page_pool: bfloat16 [96, 128, 4096], P('req', None, 'mlp'), may hold values from -100 to 100
- page_table: int32 [16, 4], P('req'), may hold values from 0 to 11, as said below
- group_index: int32 [64], P('req'), may hold values from 0 to 1
- lengths: int32 [64], P('req'), may hold values from 1 to 128, as said below
- migrants: int32 [32], P('req'), may hold values from 0 to 7, as said below
- landing: int32 [32], replicated, may hold values from 0 to 63, as said below
Outputs:
- layer_out: bfloat16 [8192, 2048], P(('req', 'mlp'))
- page_out: bfloat16 [64, 128, 4096], P('req', None, 'mlp')
Inputs may be any that keep to these rules, and one draw needn't show every extreme that they name: `adapter_ids`: the requests name exactly 16 distinct adapters in all. `lengths`: each request owner holds at least one request of 128 tokens. `page_table`: the 8 entries of one owner's rows are distinct. `migrants`: entries m // 4 = o name 4 distinct requests of owner o. `landing`: A rearrangement of the slots (m // 4) * 8 + migrants[m] of all migrating requests; the 4 requests of one owner land on 4 distinct other owners, and every owner receives exactly 4 of them.
All inputs are finite; a program needn't handle non-finite values.
Results may differ from a plain program's by a relative error of at most 0.013.
The roundings to bfloat16 on the way count: a program that leaves them out, or rounds other values in their place, can miss the bound.
Values may be sent and summed in bfloat16 or wider, within the bound.
A program may use at most 192 MiB of HBM per device.

v0:
```python
import math
import jax
import jax.numpy as jnp
from jax import lax
from jax.sharding import PartitionSpec as P

HEADS = 16
HD = 128
ADAPTERS = 64
EPS = 1e-05


def layer_norm(values, gain):
    values = values.astype(jnp.float32)
    mean = jnp.mean(values, axis=-1, keepdims=True)
    centred = values - mean
    variance = jnp.mean(centred * centred, axis=-1, keepdims=True)
    return (centred * lax.rsqrt(variance + EPS) * gain).astype(jnp.bfloat16)


def gelu_tanh(value):
    return 0.5 * value * (1.0 + jnp.tanh(0.7978845608 * (value + 0.044715 * value * value * value)))


def attend(queries, keys, values, prefix_keys, prefix_values, lens, slopes):
    scale = 1.0 / math.sqrt(queries.shape[-1])
    own_len = queries.shape[1]
    pre_len = prefix_keys.shape[1]
    s_pre = (
        jnp.einsum("rihe,rphe->rhip", queries, prefix_keys, preferred_element_type=jnp.float32)
        * scale
    )
    s_own = jnp.einsum("rihe,rjhe->rhij", queries, keys, preferred_element_type=jnp.float32) * scale
    own_pos = jnp.arange(own_len).astype(jnp.float32)
    pre_pos = jnp.arange(pre_len).astype(jnp.float32)
    s_pre = (
        s_pre
        - slopes[None, :, None, None]
        * ((pre_len + own_pos)[:, None] - pre_pos[None, :])[None, None]
    )
    s_own = s_own - slopes[None, :, None, None] * (own_pos[:, None] - own_pos[None, :])[None, None]
    steps = jnp.arange(own_len, dtype=jnp.int32)
    allowed = (steps[None, :] <= steps[:, None])[None, None] & (
        steps[None, None, None, :] < lens[:, None, None, None]
    )
    s_own = jnp.where(allowed, s_own, -jnp.inf)
    top = jnp.maximum(jnp.max(s_pre, axis=-1), jnp.max(s_own, axis=-1))[..., None]
    e_pre = jnp.exp(s_pre - top)
    e_own = jnp.exp(s_own - top)
    total = jnp.sum(e_pre, axis=-1, keepdims=True) + jnp.sum(e_own, axis=-1, keepdims=True)
    w_pre = (e_pre / total).astype(jnp.bfloat16)
    w_own = (e_own / total).astype(jnp.bfloat16)
    mixed = jnp.einsum("rhip,rphe->rihe", w_pre, prefix_values, preferred_element_type=jnp.float32)
    mixed = mixed + jnp.einsum("rhij,rjhe->rihe", w_own, values, preferred_element_type=jnp.float32)
    return mixed.astype(jnp.bfloat16)


def shards(
    tokens,
    first_gain,
    joined_weight,
    dense_weight,
    adapter_down,
    adapter_up,
    adapter_ids,
    adapter_rows,
    second_gain,
    up_weight,
    down_weight,
    page_pool,
    page_table,
    group_index,
    lengths,
    migrants,
    landing,
):
    mlp_count = lax.axis_size("mlp")
    req_index = lax.axis_index("req")
    mlp_index = lax.axis_index("mlp")
    requests = lengths.shape[0]
    slot = tokens.shape[0] // requests
    local_heads = joined_weight.shape[1] // (3 * HD)
    row_share = tokens.shape[0] // mlp_count
    own_requests = requests // mlp_count
    normed = layer_norm(tokens, first_gain)
    joined = jnp.dot(normed, joined_weight, preferred_element_type=jnp.float32).astype(jnp.bfloat16)
    joined = joined.reshape(requests, slot, local_heads, 3, HD)
    valid = jnp.arange(slot, dtype=jnp.int32)[None, :] < lengths[:, None]
    fresh = joined[:, :, :, 1:, :].reshape(requests, slot, local_heads * 2 * HD)
    fresh = jnp.where(valid[:, :, None], fresh, jnp.zeros((), jnp.bfloat16))
    pages = page_table[group_index]
    pool_view = page_pool.reshape(page_pool.shape[0], page_pool.shape[1], local_heads, 2, HD)
    prefix = pool_view[pages].reshape(
        requests, pages.shape[1] * page_pool.shape[1], local_heads, 2, HD
    )
    head_pos = (mlp_index * local_heads + jnp.arange(local_heads, dtype=jnp.int32)).astype(
        jnp.float32
    )
    slopes = jnp.exp2(-8.0 * (head_pos + 1.0) / HEADS)
    attended = attend(
        joined[:, :, :, 0],
        joined[:, :, :, 1],
        joined[:, :, :, 2],
        prefix[:, :, :, 0],
        prefix[:, :, :, 1],
        lengths,
        slopes,
    )
    attended_req = attended.reshape(requests, slot, local_heads * HD)
    local_ids = lax.dynamic_slice_in_dim(adapter_ids, req_index * requests, requests)
    every_down, every_up = (
        lax.all_gather(adapter_down, "req", axis=0, tiled=True),
        lax.all_gather(adapter_up, "req", axis=0, tiled=True),
    )
    table_rows = adapter_rows[local_ids]
    pick = (table_rows[:, None] == jnp.arange(ADAPTERS, dtype=jnp.int32)[None, :]).astype(
        jnp.bfloat16
    )
    chosen_down = jnp.einsum(
        "ra,akd->rkd", pick, every_down, preferred_element_type=jnp.float32
    ).astype(jnp.bfloat16)
    chosen_up = jnp.einsum(
        "ra,akd->rkd", pick, every_up, preferred_element_type=jnp.float32
    ).astype(jnp.bfloat16)
    dense_part = jnp.dot(
        attended.reshape(requests * slot, local_heads * HD),
        dense_weight,
        preferred_element_type=jnp.float32,
    )
    low_part = jnp.einsum(
        "rsd,rkd->rsk", attended_req, chosen_down, preferred_element_type=jnp.float32
    )
    low_part = low_part.reshape(requests * slot, low_part.shape[2])
    dense, low = (
        lax.psum_scatter(
            dense_part.astype(jnp.bfloat16), "mlp", scatter_dimension=0, tiled=True
        ).astype(jnp.float32),
        lax.psum_scatter(
            low_part.astype(jnp.bfloat16), "mlp", scatter_dimension=0, tiled=True
        ).astype(jnp.float32),
    )
    low = low.astype(jnp.bfloat16).reshape(own_requests, slot, low.shape[1])
    own_up = lax.dynamic_slice_in_dim(chosen_up, mlp_index * own_requests, own_requests)
    delta = jnp.einsum("rsk,rkd->rsd", low, own_up, preferred_element_type=jnp.float32).reshape(
        row_share, tokens.shape[1]
    )
    own_tokens = lax.dynamic_slice_in_dim(tokens, mlp_index * row_share, row_share)
    residual = (own_tokens.astype(jnp.float32) + dense + delta).astype(jnp.bfloat16)
    normed_two = layer_norm(residual, second_gain)
    expanded = gelu_tanh(
        jnp.dot(
            lax.all_gather(normed_two, "mlp", axis=0, tiled=True),
            up_weight,
            preferred_element_type=jnp.float32,
        )
    ).astype(jnp.bfloat16)
    feed = lax.psum_scatter(
        jnp.dot(expanded, down_weight, preferred_element_type=jnp.float32).astype(jnp.bfloat16),
        "mlp",
        scatter_dimension=0,
        tiled=True,
    ).astype(jnp.float32)
    own_valid = lax.dynamic_slice_in_dim(valid.reshape(-1), mlp_index * row_share, row_share)
    layer_out = jnp.where(
        own_valid[:, None], residual.astype(jnp.float32) + feed, jnp.zeros((), jnp.float32)
    ).astype(jnp.bfloat16)
    flat = fresh.reshape(requests, -1)
    moving = flat[migrants]
    own_slots = req_index * requests + jnp.arange(requests, dtype=jnp.int32)
    lands_here = landing[None, :] == own_slots[:, None]
    arrived = lax.all_gather(moving, "req", axis=0, tiled=True)
    matching = lands_here.astype(jnp.bfloat16)
    picked = jnp.dot(matching, arrived, preferred_element_type=jnp.float32).astype(jnp.bfloat16)
    moved_in = jnp.any(lands_here, axis=1)
    page_out = jnp.where(moved_in[:, None], picked, flat).reshape(
        requests, slot, flat.shape[1] // slot
    )
    return (layer_out, page_out)


def solution(mesh):
    return jax.shard_map(
        shards,
        mesh=mesh,
        in_specs=(
            P("req", None),
            P(),
            P(None, "mlp"),
            P("mlp", None),
            P("req", None, "mlp"),
            P("req", None, None),
            P(),
            P(),
            P(),
            P(None, "mlp"),
            P("mlp", None),
            P("req", None, "mlp"),
            P("req", None),
            P("req"),
            P("req"),
            P("req"),
            P(),
        ),
        out_specs=(P(("req", "mlp"), None), P("req", None, "mlp")),
        check_vma=False,
    )
```

profile of v0, /device:TPU:0, one launch (start us, length us, event | category | flops | bytes accessed | tf_op | source)
XLA Modules:
  0.0 414.1 jit_solution(13141839488661226684)
XLA Ops:
  9.1 2.2 copy.129
  13.4 3.0 convert_reduce_fusion
  18.1 10.7 %fusion.30 = bf16[1024,1536]{1,0:T(8,128)(2,1)} fusion(bf16[2048,1536]{1,0:T(8,128)(2,1)} %param.19, bf16[1024,2048]{1,0:T(8,128)(2,1)S(1)} %copy-done.4, f32[2048]{0:T(1024)S(1)} %copy-done.12, f32[1024]{0:T(1024)S(1)} %add_rsqrt_fusion, f32[1024]{0:T(1024)S(1)} %broadcast_multiply_fusion.2), kind=kOutput, calls=%fused_computation.39 | convolution fusion | flops 6454509568 | bytes 13647872 | tf_op jit(solution)/shard_map/dot_general | solution.py:86
  28.9 4.6 %copy.112 = bf16[12,128,1024]{1,2,0:T(8,128)(2,1)} copy(bf16[12,128,1024]{2,1,0:T(8,128)(2,1)} %param.28) | data formatting | bytes 6291456 | tf_op args[11]
  33.6 4.6 %copy.115 = bf16[12,128,4,2,128]{4,1,3,2,0:T(8,128)(2,1)} copy(bf16[12,128,4,2,128]{1,4,3,2,0:T(8,128)(2,1)} %bitcast.87) | data formatting | bytes 6291456 | tf_op jit(solution)/shard_map/reshape | solution.py:92
  38.2 6.9 %gather_fusion.1 = bf16[32,128,4,2,128]{4,1,3,2,0:T(8,128)(2,1)} fusion(bf16[12,128,4,2,128]{4,1,3,2,0:T(8,128)(2,1)} %copy.115, s32[1024]{0:T(1024)S(1)} %pad_clamp_fusion.2), kind=kCustom, calls=%fused_computation.1 | custom fusion | bytes 16777344 | tf_op jit(solution)/shard_map/gather | solution.py:93
  45.1 10.4 %copy.116 = bf16[32,128,4,2,128]{4,1,0,3,2:T(8,128)(2,1)} copy(bf16[32,128,4,2,128]{4,1,3,2,0:T(8,128)(2,1)} %gather_fusion.1) | data formatting | bytes 16777216 | tf_op jit(solution)/shard_map/gather | solution.py:93
  55.4 4.7 %copy.118 = bf16[1024,1536]{0,1:T(8,128)(2,1)} copy(bf16[1024,1536]{1,0:T(8,128)(2,1)} %fusion.30) | data formatting | bytes 6291456 | tf_op jit(solution)/shard_map/convert_element_type | solution.py:86
  60.2 2.9 copy.144
  68.3 2.4 copy.140
  70.7 5.9 %fusion.70 = (bf16[8,512,4,1,128]{4,1,0,3,2:T(8,128)(2,1)}, bf16[8,512,4,1,128]{4,1,0,3,2:T(8,128)(2,1)}) fusion(bf16[8,512,4,2,128]{4,1,0,3,2:T(8,128)(2,1)} %bitcast.83), kind=kLoop, calls=%fused_computation.116 | loop fusion | bytes 16777216 | tf_op jit(solution)/shard_map/slice | solution.py:104
  76.7 6.4 %copy.137 = bf16[8,512,4,1,128]{1,4,2,0,3:T(8,128)(2,1)} copy(bf16[8,512,4,1,128]{4,1,0,3,2:T(8,128)(2,1)} %get-tuple-element.17) | data formatting | bytes 8388608
  83.9 2.5 fusion.73
  88.3 2.5 fusion.12
  90.9 3.5 fusion.18
  100.0 5.6 %convolution_convert_fusion.1 = bf16[1024,2048]{1,0:T(8,128)(2,1)} fusion(bf16[512,2048]{1,0:T(8,128)(2,1)S(1)} %copy-done, bf16[64,8,8,128]{3,2,1,0:T(8,128)(2,1)} %bitcast.93), kind=kOutput, calls=%fused_computation.40 | convolution fusion | flops 2149580800 | bytes 7340032 | tf_op jit(solution)/shard_map/dot_general | solution.py:125
  107.5 3.2 copy.133
  116.2 1.8 gather_fusion.4
  118.0 8.8 %all-gather.8.cloned.1.call-done = bf16[64,16,2048]{2,0,1:T(8,128)(2,1)} async-done(((bf16[8,16,2048]{2,0,1:T(8,128)(2,1)}), bf16[64,16,2048]{2,0,1:T(8,128)(2,1)}) %all-gather.8.cloned.1.call-update) | async-done | bytes 4194320 | tf_op jit(solution)/shard_map/all_gather | solution.py:113
  126.8 2.9 fusion.56
  129.9 17.0 %reduce-scatter.6.cloned.1.call-done = bf16[256,16]{0,1:T(8,128)(2,1)} async-done(((bf16[1024,16]{0,1:T(8,128)(2,1)}), bf16[256,16]{0,1:T(8,128)(2,1)}) %reduce-scatter.6.cloned.1.call-update) | async-done | bytes 8208 | tf_op jit(solution)/shard_map/reduce_scatter | solution.py:138
  148.0 45.9 %reduce-scatter.4.cloned.1.call-done = bf16[256,2048]{1,0:T(8,128)(2,1)} async-done(((bf16[1024,2048]{1,0:T(8,128)(2,1)}), bf16[256,2048]{1,0:T(8,128)(2,1)}) %reduce-scatter.4.cloned.1.call-update) | async-done | bytes 1048592 | tf_op jit(solution)/shard_map/reduce_scatter | solution.py:135
  193.9 2.2 convert_reduce_fusion.1
  198.0 2.7 maximum_bitcast_fusion
  200.8 31.8 %all-gather.10.cloned.1.call-done = bf16[1024,2048]{1,0:T(8,128)(2,1)} async-done(((bf16[256,2048]{1,0:T(8,128)(2,1)}), bf16[1024,2048]{1,0:T(8,128)(2,1)}) %all-gather.10.cloned.1.call-update) | async-done | bytes 4194320 | tf_op jit(solution)/shard_map/all_gather | solution.py:152
  232.6 25.4 %fusion.27 = bf16[1024,2048]{1,0:T(8,128)(2,1)} fusion(bf16[2048,2048]{1,0:T(8,128)(2,1)} %param.27, bf16[1024,2048]{1,0:T(8,128)(2,1)} %all-gather.10.cloned.1.call-done, bf16[2048,2048]{1,0:T(8,128)(2,1)} %param.26), kind=kOutput, calls=%fused_computation.38 | convolution fusion | flops 17200840704 | bytes 25165824 | tf_op jit(solution)/shard_map/dot_general | solution.py:158
  258.8 100.7 %all-gather.12.cloned.1.call-done = bf16[8,4,131072]{2,1,0:T(4,128)(2,1)} async-done(((bf16[1,4,131072]{2,1,0:T(4,128)(2,1)}), bf16[8,4,131072]{2,1,0:T(4,128)(2,1)}) %all-gather.12.cloned.1.call-update) | async-done | bytes 8388624 | tf_op jit(solution)/shard_map/all_gather | solution.py:171
  359.5 7.7 %reshape.302 = bf16[32,131072]{1,0:T(8,128)(2,1)} reshape(bf16[8,4,131072]{2,1,0:T(4,128)(2,1)} %all-gather.12.cloned.1.call-done) | data formatting | bytes 16777216
  367.3 6.7 %fusion = bf16[8,131072]{1,0:T(8,128)(2,1)S(1)} fusion(bf16[8,131072]{1,0:T(8,128)(2,1)} %copy-done.5, bf16[32,131072]{1,0:T(8,128)(2,1)} %reshape.302, pred[8]{0:T(512)(128)(4,1)S(1)} %compare_reduce_fusion, s32[32]{0:T(128)S(1)} %copy-done.10, s32[8]{0:T(128)S(1)} %iota_add_fusion), kind=kOutput, calls=%fused_computation.6 | convolution fusion | flops 69206272 | bytes 12583080 | tf_op jit(solution)/shard_map/dot_general | solution.py:173
  374.0 2.5 copy.134
  376.4 28.3 %reduce-scatter.8.cloned.1.call-done = bf16[256,2048]{1,0:T(8,128)(2,1)} async-done(((bf16[1024,2048]{1,0:T(8,128)(2,1)}), bf16[256,2048]{1,0:T(8,128)(2,1)}) %reduce-scatter.8.cloned.1.call-update) | async-done | bytes 1048592 | tf_op jit(solution)/shard_map/reduce_scatter | solution.py:157
  404.8 2.5 fusion.39
  (96 shorter events, 30.7 us)
Async XLA Ops:
  7.2 92.8 %copy-start = (bf16[512,2048]{1,0:T(8,128)(2,1)S(1)}, bf16[512,2048]{1,0:T(8,128)(2,1)}, u32[]{:S(2)}) copy-start(bf16[512,2048]{1,0:T(8,128)(2,1)} %param.20) | copy-start | bytes 6291460
  7.2 90.3 %all-gather.6.cloned.1.call-start = ((), (), s32[]{:S(2)}) async-start(), calls=%async_computation.4 | async-start | bytes 1179648 | tf_op jit(solution)/shard_map/all_gather | solution.py:112
  9.0 117.8 %all-gather.8.cloned.1.call-start = ((), (), s32[]{:S(2)}) async-start(), calls=%async_computation.6 | async-start | bytes 4718592 | tf_op jit(solution)/shard_map/all_gather | solution.py:113
  11.3 135.6 %reduce-scatter.6.cloned.1.call-start = ((), (), s32[]{:S(2)}) async-start(), calls=%async_computation.5 | async-start | bytes 40960 | tf_op jit(solution)/shard_map/reduce_scatter | solution.py:138
  13.4 3.4 copy-start.4
  13.4 4.7 %copy-start.12 = (f32[2048]{0:T(1024)S(1)}, f32[2048]{0:T(1024)}, u32[]{:S(2)}) copy-start(f32[2048]{0:T(1024)} %param.18) | copy-start | bytes 24580
  63.1 1.7 copy-start.3
  76.7 6.5 %copy-start.11 = (s32[8]{0:T(128)S(1)}, s32[8]{0:T(128)}, u32[]{:S(2)}) copy-start(s32[8]{0:T(128)} %param.31) | copy-start | bytes 100
  83.1 3.3 copy-start.6
  88.3 2.5 copy-start.7
  90.9 3.5 copy-start.8
  94.4 2.5 copy-start.2
  100.0 94.0 %reduce-scatter.4.cloned.1.call-start = ((), (), s32[]{:S(2)}) async-start(), calls=%async_computation.3 | async-start | bytes 5242880 | tf_op jit(solution)/shard_map/reduce_scatter | solution.py:135
  105.6 127.0 %all-gather.10.cloned.1.call-start = ((), (), s32[]{:S(2)}) async-start(), calls=%async_computation.7 | async-start | bytes 5242880 | tf_op jit(solution)/shard_map/all_gather | solution.py:152
  105.6 5.1 %copy-start.13 = (s32[4]{0:T(128)S(1)}, s32[4]{0:T(128)}, u32[]{:S(2)}) copy-start(s32[4]{0:T(128)} %param.32) | copy-start | bytes 52
  112.9 1.3 copy-start.5
  129.9 66.7 %copy-start.9 = (f32[2048]{0:T(1024)S(1)}, f32[2048]{0:T(1024)}, u32[]{:S(2)}) copy-start(f32[2048]{0:T(1024)} %param.25) | copy-start | bytes 24580
  198.0 161.6 %all-gather.12.cloned.1.call-start = ((), (), s32[]{:S(2)}) async-start(), calls=%async_computation.9 | async-start | bytes 9437184 | tf_op jit(solution)/shard_map/all_gather | solution.py:171
  200.7 204.0 %reduce-scatter.8.cloned.1.call-start = ((), (), s32[]{:S(2)}) async-start(), calls=%async_computation.8 | async-start | bytes 5242880 | tf_op jit(solution)/shard_map/reduce_scatter | solution.py:157
  258.0 0.7 copy-start.10
  367.3 40.0 %copy-start.1 = (bf16[512,2048]{1,0:T(8,128)(2,1)S(1)}, bf16[512,2048]{1,0:T(8,128)(2,1)}, u32[]{:S(2)}) copy-start(bf16[512,2048]{1,0:T(8,128)(2,1)} %param.20) | copy-start | bytes 6291460
Sparse Core Ops, SparseCore 0:
  10.1 42.2 all-gather.5
  54.5 72.2 all-gather.7
  129.2 17.6 reduce-scatter.5
  149.4 44.4 reduce-scatter.3
  198.1 34.4 all-gather.9
  234.6 124.9 all-gather.11
  362.0 42.6 reduce-scatter.7
where the time goes:
time: 415 us; the launch traced here: 414 us
  waiting for transfers between devices  233 us (56%)
  local copies, waits for them, and re-layouts  84.5 us (20%)
  matrix products  62.4 us (15%)
  other arithmetic  19.8 us (5%)
  between operations  14.5 us (3%)
    all_gather x1, waiting for transfers between devices, shards(): arrived = lax.all_gather(moving, 'req', axis=0, tiled=True)  101 us
    reduce_scatter x1, waiting for transfers between devices, shards(): lax.psum_scatter(dense_part.astype(jnp.bfloat16), 'mlp', scatter_dimensio...  45.9 us
    unnamed x37, local copies, waits for them, and re-layouts  36.4 us
    all_gather x1, waiting for transfers between devices, shards(): lax.all_gather(normed_two, 'mlp', axis=0, tiled=True)  31.8 us
    reduce_scatter x1, waiting for transfers between devices, shards(): lax.psum_scatter(jnp.dot(expanded, down_weight, preferred_element_type=jn...  28.3 us
    dot_general x1, matrix products, shards(): jnp.dot(expanded, down_weight, preferred_element_type=jnp.float32)  25.4 us
    gather x2, local copies, waits for them, and re-layouts, shards(): pool_view[pages]  17.2 us
    reduce_scatter x1, waiting for transfers between devices, shards(): lax.psum_scatter(low_part.astype(jnp.bfloat16), 'mlp', scatter_dimension=...  17 us
  transfers between devices with their start and end apart: 7, of which 6 were waited for; matrix products, arithmetic and copies ran while one was open for 37% of the time, Pallas kernels for 0%

commit v1 on v0

--- a/solution.py
+++ b/solution.py
@@ -8,6 +8,28 @@
 HD = 128
 ADAPTERS = 64
 EPS = 1e-05
+
+
+def in_order(pieces, dim):
+    pieces = jnp.moveaxis(pieces, 0, dim)
+    dims = pieces.shape
+    return pieces.reshape(*dims[:dim], dims[dim] * dims[dim + 1], *dims[dim + 2 :])
+
+
+def gather_around(value, axis, dim):
+    size = lax.axis_size(axis)
+    pairs = [(i, (i + 1) % size) for i in range(size)]
+    back = [(b, a) for a, b in pairs]
+    lower, upper = ([], [])
+    for step in range(size - 1):
+        if step % 2 == 0:
+            lower.append(lax.ppermute(lower[-1] if lower else value, axis, pairs))
+        else:
+            upper.append(lax.ppermute(upper[-1] if upper else value, axis, back))
+    tiles = jnp.stack([*lower[::-1], value, *upper])
+    shift = lax.axis_index(axis) - len(lower)
+    tiles = tiles[(jnp.arange(size) - shift) % size]
+    return in_order(tiles, dim)
 
 
 def layer_norm(values, gain):
@@ -148,11 +170,7 @@
     residual = (own_tokens.astype(jnp.float32) + dense + delta).astype(jnp.bfloat16)
     normed_two = layer_norm(residual, second_gain)
     expanded = gelu_tanh(
-        jnp.dot(
-            lax.all_gather(normed_two, "mlp", axis=0, tiled=True),
-            up_weight,
-            preferred_element_type=jnp.float32,
-        )
+        jnp.dot(gather_around(normed_two, "mlp", 0), up_weight, preferred_element_type=jnp.float32)
     ).astype(jnp.bfloat16)
     feed = lax.psum_scatter(
         jnp.dot(expanded, down_weight, preferred_element_type=jnp.float32).astype(jnp.bfloat16),

time: 415 us -> 380 us (0.916)
  waiting for transfers between devices: 233 us -> 186 us
    all_gather x1, waiting for transfers between devices: 101 us -> 48.9 us  [shards(): arrived = lax.all_gather(moving, 'req', axis=0, tiled=True)]
    ppermute x0 -> x3, waiting for transfers between devices: none -> 37.4 us  [the longest x2 37.4 us: gather_around(): lower.append(lax.ppermute(lower[-1] if lower else value, axis, pairs))]
    all_gather x1 -> x0, waiting for transfers between devices: 31.8 us -> none  [shards(): lax.all_gather(normed_two, 'mlp', axis=0, tiled=True)]
    gather x0 -> x1, local copies, waits for them, and re-layouts: none -> 4.94 us  [gather_around(): tiles = tiles[(jnp.arange(size) - shift) % size]]
  transfers between devices with their start and end apart: 7 -> 9, of which waited for: 6 -> 7; matrix products, arithmetic and copies ran while one was open for 37% -> 44% of each run, Pallas kernels for 0% -> 0%
where the time goes in v1:
time: 380 us; the launch traced here: 376 us
  waiting for transfers between devices  186 us (49%)
  local copies, waits for them, and re-layouts  87.9 us (23%)
  matrix products  63.7 us (17%)
  other arithmetic  21.7 us (6%)
  between operations  14.7 us (4%)
    all_gather x1, waiting for transfers between devices, shards(): arrived = lax.all_gather(moving, 'req', axis=0, tiled=True)  48.9 us
    reduce_scatter x1, waiting for transfers between devices, shards(): lax.psum_scatter(dense_part.astype(jnp.bfloat16), 'mlp', scatter_dimensio...  45.9 us
    ppermute x2, waiting for transfers between devices, gather_around(): lower.append(lax.ppermute(lower[-1] if lower else value, axis, pairs))  37.4 us
    unnamed x37, local copies, waits for them, and re-layouts  36.3 us
    reduce_scatter x1, waiting for transfers between devices, shards(): lax.psum_scatter(jnp.dot(expanded, down_weight, preferred_element_type=jn...  28.3 us
    dot_general x1, matrix products, shards(): jnp.dot(expanded, down_weight, preferred_element_type=jnp.float32)  26.5 us
    gather x2, local copies, waits for them, and re-layouts, shards(): pool_view[pages]  17.2 us
    reduce_scatter x1, waiting for transfers between devices, shards(): lax.psum_scatter(low_part.astype(jnp.bfloat16), 'mlp', scatter_dimension=...  17 us
  transfers between devices with their start and end apart: 9, of which 7 were waited for; matrix products, arithmetic and copies ran while one was open for 44% of the time, Pallas kernels for 0%

profile of v1, /device:TPU:0, one launch (start us, length us, event | category | flops | bytes accessed | tf_op | source)
XLA Modules:
  0.0 376.1 jit_solution(2110495141836077701)
XLA Ops:
  13.4 3.0 convert_reduce_fusion
  18.1 11.0 %fusion.30 = bf16[1024,1536]{1,0:T(8,128)(2,1)} fusion(bf16[2048,1536]{1,0:T(8,128)(2,1)} %param.19, bf16[1024,2048]{1,0:T(8,128)(2,1)S(1)} %copy-done.4, f32[2048]{0:T(1024)S(1)} %copy-done.12, f32[1024]{0:T(1024)S(1)} %add_rsqrt_fusion, f32[1024]{0:T(1024)S(1)} %broadcast_multiply_fusion.2), kind=kOutput, calls=%fused_computation.41 | convolution fusion | flops 6454509568 | bytes 13647872 | tf_op jit(solution)/shard_map/dot_general | solution.py:108
  29.2 4.6 %copy.112 = bf16[12,128,1024]{1,2,0:T(8,128)(2,1)} copy(bf16[12,128,1024]{2,1,0:T(8,128)(2,1)} %param.28) | data formatting | bytes 6291456 | tf_op args[11]
  33.9 4.6 %copy.115 = bf16[12,128,4,2,128]{4,1,3,2,0:T(8,128)(2,1)} copy(bf16[12,128,4,2,128]{1,4,3,2,0:T(8,128)(2,1)} %bitcast.95) | data formatting | bytes 6291456 | tf_op jit(solution)/shard_map/reshape | solution.py:114
  38.5 6.9 %gather_fusion.1 = bf16[32,128,4,2,128]{4,1,3,2,0:T(8,128)(2,1)} fusion(bf16[12,128,4,2,128]{4,1,3,2,0:T(8,128)(2,1)} %copy.115, s32[1024]{0:T(1024)S(1)} %pad_clamp_fusion.3), kind=kCustom, calls=%fused_computation.1 | custom fusion | bytes 16777344 | tf_op jit(solution)/shard_map/gather | solution.py:115
  45.4 10.4 %copy.116 = bf16[32,128,4,2,128]{4,1,0,3,2:T(8,128)(2,1)} copy(bf16[32,128,4,2,128]{4,1,3,2,0:T(8,128)(2,1)} %gather_fusion.1) | data formatting | bytes 16777216 | tf_op jit(solution)/shard_map/gather | solution.py:115
  55.8 4.7 %copy.118 = bf16[1024,1536]{0,1:T(8,128)(2,1)} copy(bf16[1024,1536]{1,0:T(8,128)(2,1)} %fusion.30) | data formatting | bytes 6291456 | tf_op jit(solution)/shard_map/convert_element_type | solution.py:108
  60.5 2.9 copy.144
  68.6 2.4 copy.140
  71.0 5.9 %fusion.72 = (bf16[8,512,4,1,128]{4,1,0,3,2:T(8,128)(2,1)}, bf16[8,512,4,1,128]{4,1,0,3,2:T(8,128)(2,1)}) fusion(bf16[8,512,4,2,128]{4,1,0,3,2:T(8,128)(2,1)} %bitcast.91), kind=kLoop, calls=%fused_computation.125 | loop fusion | bytes 16777216 | tf_op jit(solution)/shard_map/slice | solution.py:126
  76.9 6.4 %copy.137 = bf16[8,512,4,1,128]{1,4,2,0,3:T(8,128)(2,1)} copy(bf16[8,512,4,1,128]{4,1,0,3,2:T(8,128)(2,1)} %get-tuple-element.17) | data formatting | bytes 8388608
  84.2 2.5 fusion.75
  88.6 2.5 fusion.12
  91.1 3.5 fusion.18
  100.3 5.6 %convolution_convert_fusion.1 = bf16[1024,2048]{1,0:T(8,128)(2,1)} fusion(bf16[512,2048]{1,0:T(8,128)(2,1)S(1)} %copy-done, bf16[64,8,8,128]{3,2,1,0:T(8,128)(2,1)} %bitcast.102), kind=kOutput, calls=%fused_computation.42 | convolution fusion | flops 2149580800 | bytes 7340032 | tf_op jit(solution)/shard_map/dot_general | solution.py:147
  107.8 3.2 copy.133
  118.3 8.5 %all-gather.7.cloned.1.call-done = bf16[64,16,2048]{2,0,1:T(8,128)(2,1)} async-done(((bf16[8,16,2048]{2,0,1:T(8,128)(2,1)}), bf16[64,16,2048]{2,0,1:T(8,128)(2,1)}) %all-gather.7.cloned.1.call-update) | async-done | bytes 4194320 | tf_op jit(solution)/shard_map/all_gather | solution.py:135
  126.8 2.9 fusion.56
  129.9 17.0 %reduce-scatter.6.cloned.1.call-done = bf16[256,16]{0,1:T(8,128)(2,1)} async-done(((bf16[1024,16]{0,1:T(8,128)(2,1)}), bf16[256,16]{0,1:T(8,128)(2,1)}) %reduce-scatter.6.cloned.1.call-update) | async-done | bytes 8208 | tf_op jit(solution)/shard_map/reduce_scatter | solution.py:160
  148.0 45.9 %reduce-scatter.4.cloned.1.call-done = bf16[256,2048]{1,0:T(8,128)(2,1)} async-done(((bf16[1024,2048]{1,0:T(8,128)(2,1)}), bf16[256,2048]{1,0:T(8,128)(2,1)}) %reduce-scatter.4.cloned.1.call-update) | async-done | bytes 1048592 | tf_op jit(solution)/shard_map/reduce_scatter | solution.py:157
  193.9 2.2 convert_reduce_fusion.1
  198.8 23.2 %collective-permute-done = bf16[256,2048]{1,0:T(8,128)(2,1)} collective-permute-done((bf16[256,2048]{1,0:T(8,128)(2,1)S(1)}, bf16[256,2048]{1,0:T(8,128)(2,1)}, u32[]{:S(2)}, u32[]{:S(2)}) %collective-permute-start) | collective-permute-done | bytes 1048608 | tf_op jit(solution)/shard_map/ppermute | solution.py:26
  222.5 14.1 %collective-permute-done.1 = bf16[256,2048]{1,0:T(8,128)(2,1)} collective-permute-done((bf16[256,2048]{1,0:T(8,128)(2,1)}, bf16[256,2048]{1,0:T(8,128)(2,1)}, u32[]{:S(2)}, u32[]{:S(2)}) %collective-permute-start.1) | collective-permute-done | bytes 1048608 | tf_op jit(solution)/shard_map/ppermute | solution.py:26
  236.6 3.8 pad_maximum_fusion
  240.3 4.9 %gather_fusion.3 = bf16[4,256,2048]{2,1,0:T(8,128)(2,1)} fusion(bf16[4,256,2048]{2,1,0:T(8,128)(2,1)} %pad_maximum_fusion, s32[1024]{0:T(1024)S(1)} %pad_clamp_fusion.1), kind=kCustom, calls=%fused_computation.3 | custom fusion | bytes 8388624 | tf_op jit(solution)/shard_map/gather | solution.py:31
  245.3 26.5 %fusion.27 = bf16[1024,2048]{1,0:T(8,128)(2,1)} fusion(bf16[2048,2048]{1,0:T(8,128)(2,1)} %param.27, bf16[1024,2048]{1,0:T(8,128)(2,1)} %bitcast.99, bf16[2048,2048]{1,0:T(8,128)(2,1)} %param.26), kind=kOutput, calls=%fused_computation.40 | convolution fusion | flops 17200840704 | bytes 25165824 | tf_op jit(solution)/shard_map/dot_general | solution.py:176
  272.6 48.9 %all-gather.9.cloned.1.call-done = bf16[8,4,131072]{2,1,0:T(4,128)(2,1)} async-done(((bf16[1,4,131072]{2,1,0:T(4,128)(2,1)}), bf16[8,4,131072]{2,1,0:T(4,128)(2,1)}) %all-gather.9.cloned.1.call-update) | async-done | bytes 8388624 | tf_op jit(solution)/shard_map/all_gather | solution.py:189
  321.4 7.7 %reshape.363 = bf16[32,131072]{1,0:T(8,128)(2,1)} reshape(bf16[8,4,131072]{2,1,0:T(4,128)(2,1)} %all-gather.9.cloned.1.call-done) | data formatting | bytes 16777216
  329.2 6.6 %fusion = bf16[8,131072]{1,0:T(8,128)(2,1)S(1)} fusion(bf16[8,131072]{1,0:T(8,128)(2,1)} %copy-done.5, bf16[32,131072]{1,0:T(8,128)(2,1)} %reshape.363, pred[8]{0:T(512)(128)(4,1)S(1)} %compare_reduce_fusion, s32[32]{0:T(128)S(1)} %copy-done.10, s32[8]{0:T(128)S(1)} %iota_add_fusion), kind=kOutput, calls=%fused_computation.7 | convolution fusion | flops 69206272 | bytes 12583080 | tf_op jit(solution)/shard_map/dot_general | solution.py:191
  335.8 2.5 copy.134
  338.2 28.3 %reduce-scatter.8.cloned.1.call-done = bf16[256,2048]{1,0:T(8,128)(2,1)} async-done(((bf16[1024,2048]{1,0:T(8,128)(2,1)}), bf16[256,2048]{1,0:T(8,128)(2,1)}) %reduce-scatter.8.cloned.1.call-update) | async-done | bytes 1048592 | tf_op jit(solution)/shard_map/reduce_scatter | solution.py:175
  366.5 2.5 fusion.39
  (104 shorter events, 35.8 us)
Async XLA Ops:
  7.2 93.1 %copy-start = (bf16[512,2048]{1,0:T(8,128)(2,1)S(1)}, bf16[512,2048]{1,0:T(8,128)(2,1)}, u32[]{:S(2)}) copy-start(bf16[512,2048]{1,0:T(8,128)(2,1)} %param.20) | copy-start | bytes 6291460
  7.2 90.6 %all-gather.5.cloned.1.call-start = ((), (), s32[]{:S(2)}) async-start(), calls=%async_computation.4 | async-start | bytes 1179648 | tf_op jit(solution)/shard_map/all_gather | solution.py:134
  9.0 117.8 %all-gather.7.cloned.1.call-start = ((), (), s32[]{:S(2)}) async-start(), calls=%async_computation.6 | async-start | bytes 4718592 | tf_op jit(solution)/shard_map/all_gather | solution.py:135
  11.3 135.6 %reduce-scatter.6.cloned.1.call-start = ((), (), s32[]{:S(2)}) async-start(), calls=%async_computation.5 | async-start | bytes 40960 | tf_op jit(solution)/shard_map/reduce_scatter | solution.py:160
  13.4 3.4 copy-start.4
  13.4 4.7 %copy-start.12 = (f32[2048]{0:T(1024)S(1)}, f32[2048]{0:T(1024)}, u32[]{:S(2)}) copy-start(f32[2048]{0:T(1024)} %param.18) | copy-start | bytes 24580
  63.4 1.7 copy-start.3
  76.9 6.5 %copy-start.11 = (s32[8]{0:T(128)S(1)}, s32[8]{0:T(128)}, u32[]{:S(2)}) copy-start(s32[8]{0:T(128)} %param.31) | copy-start | bytes 100
  83.4 3.3 copy-start.6
  88.6 2.5 copy-start.7
  91.1 3.5 copy-start.8
  94.6 2.5 copy-start.2
  100.2 93.7 %reduce-scatter.4.cloned.1.call-start = ((), (), s32[]{:S(2)}) async-start(), calls=%async_computation.3 | async-start | bytes 5242880 | tf_op jit(solution)/shard_map/reduce_scatter | solution.py:157
  105.9 215.6 %all-gather.9.cloned.1.call-start = ((), (), s32[]{:S(2)}) async-start(), calls=%async_computation.8 | async-start | bytes 9437184 | tf_op jit(solution)/shard_map/all_gather | solution.py:189
  111.4 3.3 copy-start.13
  113.2 1.3 copy-start.5
  118.3 248.3 %reduce-scatter.8.cloned.1.call-start = ((), (), s32[]{:S(2)}) async-start(), calls=%async_computation.7 | async-start | bytes 5242880 | tf_op jit(solution)/shard_map/reduce_scatter | solution.py:175
  129.9 66.7 %copy-start.9 = (f32[2048]{0:T(1024)S(1)}, f32[2048]{0:T(1024)}, u32[]{:S(2)}) copy-start(f32[2048]{0:T(1024)} %param.25) | copy-start | bytes 24580
  197.0 25.0 %collective-permute-start = (bf16[256,2048]{1,0:T(8,128)(2,1)S(1)}, bf16[256,2048]{1,0:T(8,128)(2,1)}, u32[]{:S(2)}, u32[]{:S(2)}) collective-permute-start(bf16[256,2048]{1,0:T(8,128)(2,1)S(1)} %fusion.37), channel_id=1, source_target_pairs={{0,1},{1,2},{2,3},{3,0},{4,5},{5,6},{6,7},{7,4},{8,9},{9,10},{10,1... | collective-permute-start | bytes 3145736 | tf_op jit(solution)/shard_map/ppermute | solution.py:26
  197.0 25.4 %collective-permute-start.2 = (bf16[256,2048]{1,0:T(8,128)(2,1)S(1)}, bf16[256,2048]{1,0:T(8,128)(2,1)}, u32[]{:S(2)}, u32[]{:S(2)}) collective-permute-start(bf16[256,2048]{1,0:T(8,128)(2,1)S(1)} %fusion.37), channel_id=1, source_target_pairs={{1,0},{2,1},{3,2},{0,3},{5,4},{6,5},{7,6},{4,7},{9,8},{10,9},{11,1... | collective-permute-start | bytes 3145736 | tf_op jit(solution)/shard_map/ppermute | solution.py:28
  222.0 14.5 %collective-permute-start.1 = (bf16[256,2048]{1,0:T(8,128)(2,1)}, bf16[256,2048]{1,0:T(8,128)(2,1)}, u32[]{:S(2)}, u32[]{:S(2)}) collective-permute-start(bf16[256,2048]{1,0:T(8,128)(2,1)} %collective-permute-done), channel_id=1, source_target_pairs={{0,1},{1,2},{2,3},{3,0},{4,5},{5,6},{6,7},{7,4},{8,9},{9,10},{10,1... | collective-permute-start | bytes 3145736 | tf_op jit(solution)/shard_map/ppermute | solution.py:26
  271.7 0.7 copy-start.10
  329.2 39.9 %copy-start.1 = (bf16[512,2048]{1,0:T(8,128)(2,1)S(1)}, bf16[512,2048]{1,0:T(8,128)(2,1)}, u32[]{:S(2)}) copy-start(bf16[512,2048]{1,0:T(8,128)(2,1)} %param.20) | copy-start | bytes 6291460
Sparse Core Ops, SparseCore 0:
  10.1 42.2 all-gather.4
  54.5 72.2 all-gather.6
  129.2 17.6 reduce-scatter.5
  149.4 44.4 reduce-scatter.3
  196.5 124.9 all-gather.8
  323.8 42.6 reduce-scatter.7
